TPU v7x, 32 devices: a whole 2x2x4 slice. The times are simulated.
32 devices in a mesh: dp: 4 (over y, x), seq: 8 (over z, core).
Axes of the slice: x: 2, y: 2, z: 4, core: 2. Of those that a mesh axis runs over, the one named last changes fastest.
Arguments:
- projected: bfloat16 [4, 1024, 6144], P('dp', 'seq'), may hold values from -24 to 24
- upstream: bfloat16 [4, 1024, 2048], P('dp', 'seq'), may hold values from -6 to 6
- w_out: bfloat16 [2048, 2048], replicated, may hold values from -0.125 to 0.125
- partners: int32 [8, 3], replicated, may hold values from 0 to 7, as said below
Outputs:
- grad_projected: bfloat16 [4, 1024, 6144], P('dp', 'seq')
- grad_w_out: float32 [2048, 2048], P(None, ('dp', 'seq'))
Inputs may be any that keep to these rules, and one draw needn't show every extreme that they name: `partners`: split the 8 blocks into runs of 1 block; column r maps each run one to one onto the run that lies (r + 1) * 1 runs later, counted cyclically.
All inputs are finite; a program needn't handle non-finite values.
Results may differ from a plain program's by a relative error of at most 0.0064.
Values may be sent and summed in bfloat16 or wider, within the bound.
A program may use at most 192 MiB of HBM per device.

v0:
```python
import jax
import jax.numpy as jnp
from jax import lax
from jax.sharding import PartitionSpec as P

HD = 128
BLOCK = 128
RAND = 3


NEG_FILL = -1e30


def spread(value, axis, source):
    kept = jnp.where(lax.axis_index(axis) == source, value, 0).astype(value.dtype)
    return lax.psum(kept, axis)


def extended(block, sides, width):
    for axis, dim in sides:
        count = lax.axis_size(axis)
        forward = [(i, i + 1) for i in range(count - 1)]
        backward = [(target, source) for source, target in forward]
        low = lax.ppermute(
            lax.slice_in_dim(block, block.shape[dim] - width, None, axis=dim), axis, forward
        )
        high = lax.ppermute(lax.slice_in_dim(block, 0, width, axis=dim), axis, backward)
        block = jnp.concatenate([low, block, high], axis=dim)
    return block


def from_behind(block, axis, distance):
    devices = range(lax.axis_size(axis))
    route = [((i - distance) % len(devices), i) for i in devices]
    return lax.ppermute(block, axis, route)


def shifted(value, axis, steps):
    count = lax.axis_size(axis)
    first, last = (max(0, -steps), min(count, count - steps))
    return lax.ppermute(value, axis, [(source, source + steps) for source in range(first, last)])


def round_half(value):
    return lax.optimization_barrier(value.astype(jnp.bfloat16)).astype(jnp.float32)


def on_device(projected, upstream, w_out, partners):
    local_projected = projected[0]
    local_upstream = upstream[0]
    rows = local_projected.shape[0]
    width = w_out.shape[0]
    heads = width // HD
    scale = HD ** (-0.5)
    per_device = rows // BLOCK
    seq_devices = lax.axis_size("seq")
    dp_devices = lax.axis_size("dp")
    my_index = lax.axis_index("seq")
    block_total = per_device * seq_devices
    spacing = seq_devices // (2 * RAND + 1)
    grad_factor = (rows * seq_devices * dp_devices) ** (-0.5)
    out_grad = jnp.einsum(
        "td,cd->tc", local_upstream, w_out, preferred_element_type=jnp.float32
    ).astype(jnp.bfloat16)
    key_value = local_projected[:, width:]
    both_rows = jnp.concatenate([local_projected, out_grad], axis=1)
    edge_pieces = []
    for source, offset in ((0, 0), (seq_devices - 1, rows - BLOCK)):
        edge_pieces.append(spread(both_rows, "seq", source))
    edge_rows = jnp.stack(edge_pieces)
    edge_queries = edge_rows[:, :, :width].reshape(2, BLOCK, heads, HD)
    edge_out_grad = edge_rows[:, :, 3 * width :].reshape(2, BLOCK, heads, HD)
    own_ids = my_index * per_device + jnp.arange(per_device, dtype=jnp.int32)
    block_ids = jnp.arange(block_total, dtype=jnp.int32)
    ahead = lax.dynamic_slice_in_dim(partners, my_index * per_device, per_device, 0)
    hits = partners[:, :, None] == own_ids[None, None, :]
    behind = jnp.transpose(jnp.sum(jnp.where(hits, block_ids[:, None, None], 0), axis=0), (1, 0))
    fixed_ids = jnp.stack(
        [
            own_ids - 1,
            own_ids,
            own_ids + 1,
            jnp.zeros_like(own_ids),
            jnp.full_like(own_ids, block_total - 1),
        ],
        axis=1,
    )
    slot_ids = jnp.concatenate([fixed_ids, ahead, behind], axis=1)
    slots = slot_ids.shape[1]
    slot_range = jnp.arange(slots, dtype=jnp.int32)
    earlier = slot_range[None, None, :] < slot_range[None, :, None]
    repeated = jnp.any((slot_ids[:, :, None] == slot_ids[:, None, :]) & earlier, axis=2)
    valid = (slot_ids >= 0) & (slot_ids < block_total) & jnp.logical_not(repeated)
    is_first = own_ids == 0
    is_last = own_ids == block_total - 1
    regular = jnp.logical_not(is_first | is_last)
    rimmed = extended(key_value, (("seq", 0),), BLOCK)
    offsets = []
    for step in range(RAND):
        offsets.append((step + 1) * spacing)
        offsets.append(-(step + 1) * spacing)
    fetched = [from_behind(key_value, "seq", -offset) for offset in offsets]
    edge_kv = edge_rows[:, :, width : 3 * width].reshape(2 * BLOCK, 2 * width)
    pool_kv = jnp.concatenate(
        [key_value, rimmed[:BLOCK], rimmed[-BLOCK:], edge_kv] + fetched, axis=0
    ).reshape(-1, BLOCK, 2 * width)
    shard_ids = [
        (my_index + offset) % seq_devices * per_device + jnp.arange(per_device, dtype=jnp.int32)
        for offset in offsets
    ]
    pool_ids = jnp.concatenate(
        [own_ids, own_ids - 1, own_ids + 1, jnp.array([0, block_total - 1], jnp.int32)] + shard_ids
    )
    pool_count = pool_ids.shape[0]
    matches = slot_ids[:, :, None] == pool_ids[None, None, :]
    position = jnp.min(
        jnp.where(matches, jnp.arange(pool_count, dtype=jnp.int32)[None, None, :], pool_count),
        axis=2,
    )
    position = jnp.where(valid, position, 0)
    slot_kv = jnp.take(pool_kv, position, axis=0)
    slot_keys = slot_kv[..., :width].reshape(per_device, slots, BLOCK, heads, HD)
    slot_values = slot_kv[..., width:].reshape(per_device, slots, BLOCK, heads, HD)
    block_queries = local_projected[:, :width].reshape(per_device, BLOCK, heads, HD)
    seen = valid[:, None, None, :, None]
    scores = (
        jnp.einsum(
            "bqhd,bskhd->bhqsk", block_queries, slot_keys, preferred_element_type=jnp.float32
        )
        * scale
    )
    scores = jnp.where(seen, scores, NEG_FILL)
    row_max = jnp.max(scores, axis=(3, 4), keepdims=True)
    exponent = jnp.where(seen, jnp.exp(scores - row_max), 0.0)
    total = jnp.sum(exponent, axis=(3, 4), keepdims=True)
    weighted = jnp.einsum(
        "bhqsk,bskhd->bhqd",
        exponent.astype(jnp.bfloat16),
        slot_values,
        preferred_element_type=jnp.float32,
    )
    regular_att = weighted / total[:, :, :, :, 0]
    own_keys = key_value[:, :width].reshape(rows, heads, HD)
    own_values = key_value[:, width:].reshape(rows, heads, HD)
    edge_scores = (
        jnp.einsum("gqhd,khd->ghqk", edge_queries, own_keys, preferred_element_type=jnp.float32)
        * scale
    )
    edge_max = lax.pmax(jnp.max(edge_scores, axis=3, keepdims=True), "seq")
    edge_exp = jnp.exp(edge_scores - edge_max)
    edge_part = jnp.einsum(
        "ghqk,khd->ghqd",
        edge_exp.astype(jnp.bfloat16),
        own_values,
        preferred_element_type=jnp.float32,
    )
    edge_total, edge_summed = lax.psum((jnp.sum(edge_exp, axis=3, keepdims=True), edge_part), "seq")
    edge_att = edge_summed / edge_total
    first_mask = is_first[:, None, None, None]
    last_mask = is_last[:, None, None, None]
    attended = jnp.where(
        first_mask, edge_att[0][None], jnp.where(last_mask, edge_att[1][None], regular_att)
    )
    attended_out = jnp.transpose(attended, (0, 2, 1, 3)).reshape(rows, width).astype(jnp.bfloat16)
    column_width = local_upstream.shape[1] // (dp_devices * seq_devices)
    split_up = local_upstream.reshape(rows, dp_devices, seq_devices, column_width)
    picked_columns = lax.all_to_all(
        split_up, "seq", split_axis=2, concat_axis=0, tiled=True
    ).reshape(-1, dp_devices * column_width)
    sequence_sum = jnp.einsum(
        "tc,tk->ck",
        lax.all_gather(attended_out, "seq", axis=0, tiled=True),
        picked_columns,
        preferred_element_type=jnp.float32,
    )
    scaled_sum = (sequence_sum * grad_factor).reshape(width, dp_devices, column_width)
    grad_w_out = lax.psum_scatter(scaled_sum, "dp", scatter_dimension=1, tiled=True).reshape(
        width, column_width
    )
    block_grads = out_grad.reshape(per_device, BLOCK, heads, HD)
    grads_float = jnp.transpose(block_grads, (0, 2, 1, 3)).astype(jnp.float32)
    delta = jnp.sum(grads_float * attended, axis=3)
    probs = jnp.where(regular[:, None, None, None, None], exponent / total, 0.0)
    prob_grad = jnp.einsum(
        "bqhd,bskhd->bhqsk", block_grads, slot_values, preferred_element_type=jnp.float32
    )
    score_grad = (probs * (prob_grad - delta[:, :, :, None, None])).astype(jnp.bfloat16)
    regular_query = (
        jnp.einsum("bhqsk,bskhd->bqhd", score_grad, slot_keys, preferred_element_type=jnp.float32)
        * scale
    )
    key_term = round_half(
        jnp.einsum(
            "bhqsk,bqhd->bskhd", score_grad, block_queries, preferred_element_type=jnp.float32
        )
        * scale
    )
    value_term = round_half(
        jnp.einsum(
            "bhqsk,bqhd->bskhd",
            probs.astype(jnp.bfloat16),
            block_grads,
            preferred_element_type=jnp.float32,
        )
    )
    slot_terms = jnp.concatenate(
        [
            key_term.reshape(per_device * slots, BLOCK, width),
            value_term.reshape(per_device * slots, BLOCK, width),
        ],
        axis=2,
    )
    pool_terms = (
        jnp.zeros((pool_count, BLOCK, 2 * width), jnp.float32)
        .at[position.reshape(-1)]
        .add(slot_terms)
    )
    edge_grads_float = jnp.transpose(edge_out_grad, (0, 2, 1, 3)).astype(jnp.float32)
    edge_delta = jnp.sum(edge_grads_float * edge_att, axis=3)
    edge_probs = edge_exp / edge_total
    edge_prob_grad = jnp.einsum(
        "gqhd,khd->ghqk", edge_out_grad, own_values, preferred_element_type=jnp.float32
    )
    edge_score_grad = (edge_probs * (edge_prob_grad - edge_delta[:, :, :, None])).astype(
        jnp.bfloat16
    )
    edge_query_part = (
        jnp.einsum("ghqk,khd->gqhd", edge_score_grad, own_keys, preferred_element_type=jnp.float32)
        * scale
    )
    edge_key_term = round_half(
        jnp.einsum(
            "ghqk,gqhd->gkhd", edge_score_grad, edge_queries, preferred_element_type=jnp.float32
        )
        * scale
    )
    edge_value_term = round_half(
        jnp.einsum(
            "ghqk,gqhd->gkhd",
            edge_probs.astype(jnp.bfloat16),
            edge_out_grad,
            preferred_element_type=jnp.float32,
        )
    )
    own_terms = jnp.sum(
        jnp.concatenate(
            [edge_key_term.reshape(2, rows, width), edge_value_term.reshape(2, rows, width)], axis=2
        ),
        axis=0,
    )
    edge_query_sum, edge_terms = lax.psum(
        (edge_query_part, pool_terms[per_device + 2 : per_device + 4]), "seq"
    )
    rim_returns = [
        shifted(pool_terms[per_device + side].astype(jnp.bfloat16), "seq", direction).astype(
            jnp.float32
        )
        for side, direction in ((0, -1), (1, 1))
    ]
    key_grads = pool_terms[:per_device].reshape(rows, 2 * width) + own_terms
    key_grads = key_grads.at[rows - BLOCK :].add(rim_returns[0]).at[:BLOCK].add(rim_returns[1])
    key_grads = key_grads.at[:BLOCK].add(jnp.where(my_index == 0, edge_terms[0], 0.0))
    key_grads = key_grads.at[rows - BLOCK :].add(
        jnp.where(my_index == seq_devices - 1, edge_terms[1], 0.0)
    )
    for slot_number, offset in enumerate(offsets):
        begin = per_device + 4 + slot_number * per_device
        piece = pool_terms[begin : begin + per_device].reshape(rows, 2 * width).astype(jnp.bfloat16)
        key_grads = key_grads + from_behind(piece, "seq", offset).astype(jnp.float32)
    query_grad = jnp.where(
        first_mask,
        edge_query_sum[0][None],
        jnp.where(last_mask, edge_query_sum[1][None], regular_query),
    )
    qkv_grad = jnp.concatenate([query_grad.reshape(rows, width), key_grads], axis=1).astype(
        jnp.bfloat16
    )
    return (qkv_grad[None], grad_w_out)


def solution(mesh):
    return jax.shard_map(
        on_device,
        mesh=mesh,
        in_specs=(P("dp", "seq", None), P("dp", "seq", None), P(), P()),
        out_specs=(P("dp", "seq", None), P(None, ("dp", "seq"))),
        check_vma=False,
    )
```

profile of v0, /device:TPU:1, one launch (start us, length us, event | category | flops | bytes accessed | tf_op | source)
XLA Modules:
  0.0 860.5 jit_solution(5574201625457071976)
XLA Ops:
  9.2 3.7 collective-permute-start.7
  14.2 3.0 collective-permute-start.4
  17.3 6.4 convolution_convert_fusion
  24.8 3.7 select_bitcast_fusion
  32.5 5.4 collective-permute-done.7
  37.9 63.0 %collective-permute-start.2 = (bf16[128,4096]{0,1:T(8,128)(2,1)S(1)}, bf16[128,4096]{0,1:T(8,128)(2,1)}, u32[]{:S(2)}, u32[]{:S(2)}) collective-permute-start(bf16[128,4096]{0,1:T(8,128)(2,1)S(1)} %slice.174), channel_id=1, source_target_pairs={{1,0},{2,1},{3,2},{4,3},{5,4},{6,5},{7,6},{0,7},{9,8},{10,9},{11,1... | collective-permute-start | bytes 3145736 | tf_op jit(solution)/shard_map/ppermute | solution.py:35
  100.9 12.1 %collective-permute-done.6 = bf16[128,4096]{0,1:T(8,128)(2,1)} collective-permute-done((bf16[128,4096]{0,1:T(8,128)(2,1)S(1)}, bf16[128,4096]{0,1:T(8,128)(2,1)}, u32[]{:S(2)}, u32[]{:S(2)}) %collective-permute-start.6) | collective-permute-done | bytes 1048608 | tf_op jit(solution)/shard_map/ppermute | solution.py:35
  114.9 76.7 %collective-permute-start = (bf16[128,4096]{0,1:T(8,128)(2,1)S(1)}, bf16[128,4096]{0,1:T(8,128)(2,1)}, u32[]{:S(2)}, u32[]{:S(2)}) collective-permute-start(bf16[128,4096]{0,1:T(8,128)(2,1)S(1)} %slice.174), channel_id=1, source_target_pairs={{0,1},{1,2},{2,3},{3,4},{4,5},{5,6},{6,7},{8,9},{9,10},{10,11},{11... | collective-permute-start | bytes 3145736 | tf_op jit(solution)/shard_map/ppermute | solution.py:24
  191.7 2.3 constant_dynamic-update-slice_fusion.11
  195.1 2.3 copy.213
  197.5 2.3 copy.212
  199.7 2.3 copy.211
  202.1 2.3 copy.210
  204.4 2.3 copy.209
  206.7 2.3 copy.208
  210.5 15.5 %collective-permute-done = bf16[128,4096]{0,1:T(8,128)(2,1)} collective-permute-done((bf16[128,4096]{0,1:T(8,128)(2,1)S(1)}, bf16[128,4096]{0,1:T(8,128)(2,1)}, u32[]{:S(2)}, u32[]{:S(2)}) %collective-permute-start) | collective-permute-done | bytes 1048608 | tf_op jit(solution)/shard_map/ppermute | solution.py:24
  229.6 5.8 all-reduce.11.cloned.1.call-done
  240.2 2.8 copy.204
  244.6 25.4 %pmax.7 = f32[2,16,128]{2,0,1:T(2,128)S(1)} all-reduce(f32[2,16,128]{2,0,1:T(2,128)S(1)} %get-tuple-element.110), channel_id=1, replica_groups=mesh['dp'=4,'seq'=8] {'seq'}, use_global_device_ids=true, to_apply=%region_3.4 | all-reduce | flops 4096 | bytes 32768 | tf_op jit(solution)/shard_map/pmax | solution.py:149
  270.0 2.9 convolution_bitcast_fusion
  273.1 3.3 constant_dynamic-update-slice_fusion.8
  276.4 2.4 constant_dynamic-update-slice_fusion.7
  284.3 10.0 %gather_fusion = bf16[11,128,4096]{2,1,0:T(8,128)(2,1)} fusion(bf16[11,128,4096]{2,1,0:T(8,128)(2,1)} %bitcast.290, s32[1024]{0:T(1024)S(1)} %pad_clamp_fusion), kind=kCustom, calls=%fused_computation | custom fusion | bytes 23068716 | tf_op jit(solution)/shard_map/jit(_take)/gather | solution.py:121
  294.3 10.3 %bitcast_select_fusion = bf16[1,11,128,4096]{3,2,1,0:T(8,128)(2,1)} fusion(bf16[11,128,4096]{2,1,0:T(8,128)(2,1)} %gather_fusion, pred[11]{0:T(512)(128)(4,1)S(1)} %get-tuple-element.86), kind=kLoop, calls=%fused_computation.7 | loop fusion | flops 5767168 | bytes 23068684 | tf_op jit(solution)/shard_map/jit(_take)/select_n | solution.py:121
  304.6 11.2 %fusion.92 = (bf16[1,11,128,2048]{3,2,1,0:T(8,128)(2,1)}, bf16[1,11,128,2048]{3,2,1,0:T(8,128)(2,1)}) fusion(bf16[1,11,128,4096]{3,2,1,0:T(8,128)(2,1)} %bitcast_select_fusion), kind=kLoop, calls=%fused_computation.130 | loop fusion | bytes 23068672 | tf_op jit(solution)/shard_map/slice | solution.py:123
  315.8 8.5 copy.214
  324.3 9.5 %bitcast_reduce_fusion = (f32[16,128]{1,0:T(8,128)S(1)}, f32[16,11,128,128]{3,2,1,0:T(8,128)}) fusion(pred[11]{0:T(512)(128)(4,1)S(1)} %get-tuple-element.87, bf16[128,16,128,1]{0,2,3,1:T(8,128)(2,1)S(1)} %bitcast.309, bf16[11,128,16,128]{1,3,2,0:T(8,128)(2,1)} %bitcast.298), kind=kOutput, calls=%fused_computation.4 | convolution fusion | flops 746846208 | bytes 17833996 | tf_op jit(solution)/shard_map/bqhd,bskhd->bhqsk/dot_general | solution.py:127
  334.2 8.4 copy.217
  342.6 26.0 %psum.44 = f32[2,16,128]{2,0,1:T(2,128)S(1)} all-reduce(f32[2,16,128]{2,0,1:T(2,128)S(1)} %fusion.48), channel_id=1, replica_groups=mesh['dp'=4,'seq'=8] {'seq'}, use_global_device_ids=true, to_apply=%region_5.6 | all-reduce | flops 4096 | bytes 32768 | tf_op jit(solution)/shard_map/psum | solution.py:157
  368.7 7.2 fusion.91
  375.9 3.5 fusion.32
  379.4 10.3 %fusion.95 = (bf16[1,16,128,128]{2,3,0,1:T(8,128)(2,1)}, f32[16,128]{1,0:T(8,128)S(1)}) fusion(f32[128,2048]{0,1:T(8,128)S(1)} %copy-done.16, f32[16,128]{1,0:T(8,128)S(1)} %fusion.91, f32[16,128]{1,0:T(8,128)S(1)} %get-tuple-element.108, f32[16,11,128,128]{3,2,1,0:T(8,128)} %get-tuple-element.109, pred[11]{0:T(512)(128)(4,1)S(1)} %get-tuple-element.87, ...), kind=kOutput, calls=%fused_computation.133 | convolution fusion | flops 754186240 | bytes 20997122 | tf_op jit(solution)/shard_map/bhqsk,bskhd->bhqd/dot_general | solution.py:136
  389.7 2.1 copy.240
  393.7 8.1 all-to-all-start
  402.3 2.0 copy.293
  404.3 2.2 copy.263
  406.6 25.9 %all-to-all-done = bf16[128,4,8,64]{0,3,1,2:T(8,128)(2,1)} async-done(((bf16[128,4,8,64]{0,3,1,2:T(8,128)(2,1)}), bf16[128,4,8,64]{0,3,1,2:T(8,128)(2,1)}, u32[]{:S(2)}, u32[]{:S(2)}) %all-to-all-start) | async-done | bytes 524320 | tf_op jit(solution)/shard_map/all_to_all | solution.py:167
  432.5 2.2 copy.242
  434.7 9.1 %convert_bitcast_fusion = bf16[1,11,128,16,128]{2,4,1,3,0:T(8,128)(2,1)S(1)} fusion(bf16[128,16,128,1]{0,2,3,1:T(8,128)(2,1)} %copy.263, f32[16,128]{1,0:T(8,128)S(1)} %fusion.91, pred[]{:T(512)} %bitcast.44, f32[16,11,128,128]{3,2,1,0:T(8,128)} %get-tuple-element.109, f32[16,128]{1,0:T(8,128)S(1)} %get-tuple-element.108, ...), kind=kOutput, calls=%fused_computation.17 | convolution fusion | flops 761266176 | bytes 17842188 | tf_op jit(solution)/shard_map/bhqsk,bqhd->bskhd/dot_general | solution.py:199
  443.7 3.7 copy.234
  447.5 9.2 %multiply_convert_fusion.1 = bf16[16,128,11,128]{1,3,2,0:T(8,128)(2,1)S(1)} fusion(f32[16,128]{1,0:T(8,128)S(1)} %get-tuple-element.106, f32[16,128]{1,0:T(8,128)S(1)} %fusion.91, pred[]{:T(512)} %bitcast.44, bf16[128,16,128,1]{0,2,3,1:T(8,128)(2,1)S(1)} %copy-done.17, bf16[11,128,16,128]{1,3,2,0:T(8,128)(2,1)} %bitcast.301, ...), kind=kOutput, calls=%fused_computation.9 | convolution fusion | flops 764149760 | bytes 23617548 | tf_op jit(solution)/shard_map/bqhd,bskhd->bhqsk/dot_general | solution.py:184
  456.7 2.4 copy-done.4
  459.2 3.4 fusion.2
  462.6 8.3 copy.231
  470.8 12.6 %maximum_convert_fusion = f32[11,128,4096]{1,2,0:T(8,128)} fusion(bf16[11,128,2048]{1,2,0:T(8,128)(2,1)} %bitcast.285, bf16[11,128,2048]{1,2,0:T(8,128)(2,1)} %bitcast.286), kind=kLoop, calls=%fused_computation.2 | loop fusion | flops 23068672 | bytes 34603008 | tf_op jit(solution)/shard_map/concatenate | solution.py:206
  483.5 23.4 %copy.235 = f32[11,128,4096]{2,1,0:T(8,128)} copy(f32[11,128,4096]{1,2,0:T(8,128)} %maximum_convert_fusion) | data formatting | bytes 46137344 | tf_op jit(solution)/shard_map/concatenate | solution.py:206
  506.9 10.6 %broadcast_in_dim.154 = f32[11,128,4096]{2,1,0:T(8,128)} broadcast(f32[]{:T(128)} %constant.243.clone.1), dimensions={} | broadcast | bytes 23068676 | tf_op jit(solution)/shard_map/broadcast_in_dim | solution.py:214
  517.5 41.9 %scatter_fusion = f32[11,128,4096]{2,1,0:T(8,128)} fusion(f32[11,128,4096]{2,1,0:T(8,128)} %broadcast_in_dim.154, s32[11]{0:T(128)S(1)} %fusion.86, f32[11,128,4096]{2,1,0:T(8,128)} %copy.235), kind=kCustom, calls=%fused_computation.1 | custom fusion | flops 5767168 | bytes 69206064 | tf_op jit(solution)/shard_map/scatter-add | solution.py:216
  559.4 4.7 slice.184
  566.0 9.9 %convert.28 = bf16[11,128,4096]{2,1,0:T(8,128)(2,1)S(1)} convert(f32[11,128,4096]{2,1,0:T(8,128)} %scatter_fusion) | non-fusion elementwise | flops 5767168 | bytes 34603008 | tf_op jit(solution)/shard_map/convert.20
  577.7 3.3 slice_bitcast_fusion.8
  581.0 2.4 collective-permute-start.8
  583.5 2.6 collective-permute-start.14
  586.1 5.1 convolution_multiply_fusion
  591.2 174.6 %all-reduce.12 = bf16[2,128,16,128]{1,3,0,2:T(8,128)(2,1)} all-reduce(f32[2,128,16,128]{1,3,0,2:T(8,128)} %multiply_bitcast_fusion), channel_id=1, replica_groups=mesh['dp'=4,'seq'=8] {'seq'}, use_global_device_ids=true, to_apply=%region_8.9 | all-reduce | flops 524288 | bytes 3145728 | tf_op jit(solution)/shard_map/psum | solution.py:251
  765.9 2.7 collective-permute-start.12
  771.2 2.3 collective-permute-start.9
  773.5 2.1 fusion.36
  777.3 1.9 copy.238
  779.3 7.1 fusion.61
  787.7 30.1 %collective-permute-done.13 = bf16[128,4096]{1,0:T(8,128)(2,1)} collective-permute-done((bf16[128,4096]{1,0:T(8,128)(2,1)}, bf16[128,4096]{1,0:T(8,128)(2,1)}, u32[]{:S(2)}, u32[]{:S(2)}) %collective-permute-start.13) | collective-permute-done | bytes 1048608 | tf_op jit(solution)/shard_map/ppermute | solution.py:35
  817.7 18.2 %collective-permute-done.11 = bf16[128,4096]{1,0:T(8,128)(2,1)} collective-permute-done((bf16[128,4096]{1,0:T(8,128)(2,1)}, bf16[128,4096]{1,0:T(8,128)(2,1)}, u32[]{:S(2)}, u32[]{:S(2)}) %collective-permute-start.11) | collective-permute-done | bytes 1048608 | tf_op jit(solution)/shard_map/ppermute | solution.py:35
  835.9 9.5 %collective-permute-done.9 = bf16[128,4096]{1,0:T(8,128)(2,1)} collective-permute-done((bf16[128,4096]{1,0:T(8,128)(2,1)}, bf16[128,4096]{1,0:T(8,128)(2,1)}, u32[]{:S(2)}, u32[]{:S(2)}) %collective-permute-start.9) | collective-permute-done | bytes 1048608 | tf_op jit(solution)/shard_map/ppermute | solution.py:41
  845.4 7.1 fusion.72
  (112 shorter events, 42.1 us)
Async XLA Ops:
  7.2 228.2 %all-reduce.11.cloned.1.call-start = ((), (), s32[]{:S(2)}) async-start(), calls=%async_computation.6 | async-start | bytes 8388608 | tf_op jit(solution)/shard_map/psum | solution.py:16
  9.2 28.7 %collective-permute-start.7 = (bf16[128,4096]{0,1:T(8,128)(2,1)S(1)}, bf16[128,4096]{0,1:T(8,128)(2,1)}, u32[]{:S(2)}, u32[]{:S(2)}) collective-permute-start(bf16[128,4096]{0,1:T(8,128)(2,1)S(1)} %slice.174), channel_id=1, source_target_pairs={{5,0},{6,1},{7,2},{0,3},{1,4},{2,5},{3,6},{4,7},{13,8},{14,9},{15,... | collective-permute-start | bytes 3145736 | tf_op jit(solution)/shard_map/ppermute | solution.py:35
  12.9 100.0 %collective-permute-start.6 = (bf16[128,4096]{0,1:T(8,128)(2,1)S(1)}, bf16[128,4096]{0,1:T(8,128)(2,1)}, u32[]{:S(2)}, u32[]{:S(2)}) collective-permute-start(bf16[128,4096]{0,1:T(8,128)(2,1)S(1)} %slice.174), channel_id=1, source_target_pairs={{3,0},{4,1},{5,2},{6,3},{7,4},{0,5},{1,6},{2,7},{11,8},{12,9},{13,... | collective-permute-start | bytes 3145736 | tf_op jit(solution)/shard_map/ppermute | solution.py:35
  14.0 100.9 %collective-permute-start.5 = (bf16[128,4096]{0,1:T(8,128)(2,1)S(1)}, bf16[128,4096]{0,1:T(8,128)(2,1)}, u32[]{:S(2)}, u32[]{:S(2)}) collective-permute-start(bf16[128,4096]{0,1:T(8,128)(2,1)S(1)} %slice.174), channel_id=1, source_target_pairs={{6,0},{7,1},{0,2},{1,3},{2,4},{3,5},{4,6},{5,7},{14,8},{15,9},{8,1... | collective-permute-start | bytes 3145736 | tf_op jit(solution)/shard_map/ppermute | solution.py:35
  14.2 187.8 %collective-permute-start.4 = (bf16[128,4096]{0,1:T(8,128)(2,1)S(1)}, bf16[128,4096]{0,1:T(8,128)(2,1)}, u32[]{:S(2)}, u32[]{:S(2)}) collective-permute-start(bf16[128,4096]{0,1:T(8,128)(2,1)S(1)} %slice.174), channel_id=1, source_target_pairs={{2,0},{3,1},{4,2},{5,3},{6,4},{7,5},{0,6},{1,7},{10,8},{11,9},{12,... | collective-permute-start | bytes 3145736 | tf_op jit(solution)/shard_map/ppermute | solution.py:35
  17.3 187.1 %collective-permute-start.3 = (bf16[128,4096]{0,1:T(8,128)(2,1)S(1)}, bf16[128,4096]{0,1:T(8,128)(2,1)}, u32[]{:S(2)}, u32[]{:S(2)}) collective-permute-start(bf16[128,4096]{0,1:T(8,128)(2,1)S(1)} %slice.174), channel_id=1, source_target_pairs={{7,0},{0,1},{1,2},{2,3},{3,4},{4,5},{5,6},{6,7},{15,8},{8,9},{9,10... | collective-permute-start | bytes 3145736 | tf_op jit(solution)/shard_map/ppermute | solution.py:35
  23.7 6.3 copy-start.3
  23.8 4.8 copy-start.18
  28.5 347.5 %all-reduce.7.cloned.1.call-start = ((), (), s32[]{:S(2)}) async-start(), calls=%async_computation.2 | async-start | bytes 4194304 | tf_op jit(solution)/shard_map/psum | solution.py:157
  37.9 168.8 %collective-permute-start.2 = (bf16[128,4096]{0,1:T(8,128)(2,1)S(1)}, bf16[128,4096]{0,1:T(8,128)(2,1)}, u32[]{:S(2)}, u32[]{:S(2)}) collective-permute-start(bf16[128,4096]{0,1:T(8,128)(2,1)S(1)} %slice.174), channel_id=1, source_target_pairs={{1,0},{2,1},{3,2},{4,3},{5,4},{6,5},{7,6},{0,7},{9,8},{10,9},{11,1... | collective-permute-start | bytes 3145736 | tf_op jit(solution)/shard_map/ppermute | solution.py:35
  113.0 96.0 %collective-permute-start.1 = (bf16[128,4096]{0,1:T(8,128)(2,1)S(1)}, bf16[128,4096]{0,1:T(8,128)(2,1)}, u32[]{:S(2)}, u32[]{:S(2)}) collective-permute-start(bf16[128,4096]{0,1:T(8,128)(2,1)S(1)} %slice.174), channel_id=1, source_target_pairs={{1,0},{2,1},{3,2},{4,3},{5,4},{6,5},{7,6},{9,8},{10,9},{11,10},{12... | collective-permute-start | bytes 3145736 | tf_op jit(solution)/shard_map/ppermute | solution.py:27
  114.9 111.0 %collective-permute-start = (bf16[128,4096]{0,1:T(8,128)(2,1)S(1)}, bf16[128,4096]{0,1:T(8,128)(2,1)}, u32[]{:S(2)}, u32[]{:S(2)}) collective-permute-start(bf16[128,4096]{0,1:T(8,128)(2,1)S(1)} %slice.174), channel_id=1, source_target_pairs={{0,1},{1,2},{2,3},{3,4},{4,5},{5,6},{6,7},{8,9},{9,10},{10,11},{11... | collective-permute-start | bytes 3145736 | tf_op jit(solution)/shard_map/ppermute | solution.py:24
  240.2 32.6 %copy-start = (bf16[2,128,2048]{1,2,0:T(8,128)(2,1)}, bf16[2,128,2048]{1,2,0:T(8,128)(2,1)S(1)}, u32[]{:S(2)}) copy-start(bf16[2,128,2048]{1,2,0:T(8,128)(2,1)S(1)} %get-tuple-element.98) | copy-start | bytes 3145732
  272.8 8.2 copy-start.10
  272.9 313.3 %all-gather.2.cloned.1.call-start = ((), (), s32[]{:S(2)}) async-start(), calls=%async_computation.4 | async-start | bytes 4718592 | tf_op jit(solution)/shard_map/all_gather | solution.py:172
  273.1 5.7 copy-start.12
  273.1 6.8 copy-start.11
  273.1 9.0 %copy-start.9 = (bf16[128,4096]{1,0:T(8,128)(2,1)S(1)}, bf16[128,4096]{1,0:T(8,128)(2,1)}, u32[]{:S(2)}) copy-start(bf16[128,4096]{1,0:T(8,128)(2,1)} %copy.212) | copy-start | bytes 3145732
  276.4 6.8 copy-start.8
  315.8 8.5 copy-start.13
  368.7 7.2 copy-start.2
  375.9 3.5 copy-start.16
  393.7 38.8 %all-to-all-start = ((bf16[128,4,8,64]{0,3,1,2:T(8,128)(2,1)}), bf16[128,4,8,64]{0,3,1,2:T(8,128)(2,1)}, u32[]{:S(2)}, u32[]{:S(2)}) async-start(bf16[128,4,8,64]{0,3,1,2:T(8,128)(2,1)} %copy.241), calls=%async_computation | async-start | bytes 1048576 | tf_op jit(solution)/shard_map/all_to_all | solution.py:167
  401.8 443.6 %all-reduce.9.cloned.1.call-start = ((), (), s32[]{:S(2)}) async-start(), calls=%async_computation.3 | async-start | bytes 8388608 | tf_op jit(solution)/shard_map/psum | solution.py:251
  443.7 3.7 copy-start.17
  447.5 11.7 %copy-start.14 = (bf16[128,2048]{0,1:T(8,128)(2,1)S(1)}, bf16[128,2048]{0,1:T(8,128)(2,1)}, u32[]{:S(2)}) copy-start(bf16[128,2048]{0,1:T(8,128)(2,1)} %get-tuple-element.103) | copy-start | bytes 1572868
  456.7 2.4 copy-start.4
  564.1 289.6 %reduce-scatter.4.cloned.1.call-start = ((), (), s32[]{:S(2)}) async-start(), calls=%async_computation.5 | async-start | bytes 2621440
  566.0 10.0 %copy-start.6 = (bf16[2,16,128,128]{2,3,0,1:T(8,128)(2,1)}, bf16[2,16,128,128]{2,3,0,1:T(8,128)(2,1)S(1)}, u32[]{:S(2)}) copy-start(bf16[2,16,128,128]{2,3,0,1:T(8,128)(2,1)S(1)} %fusion.34) | copy-start | bytes 3145732
  566.0 10.0 %copy-start.5 = (bf16[128,2048]{0,1:T(8,128)(2,1)S(1)}, bf16[128,2048]{0,1:T(8,128)(2,1)}, u32[]{:S(2)}) copy-start(bf16[128,2048]{0,1:T(8,128)(2,1)} %get-tuple-element.102) | copy-start | bytes 1572868
  581.0 188.4 %collective-permute-start.8 = (bf16[128,4096]{1,0:T(8,128)(2,1)}, bf16[128,4096]{1,0:T(8,128)(2,1)}, u32[]{:S(2)}, u32[]{:S(2)}) collective-permute-start(bf16[128,4096]{1,0:T(8,128)(2,1)} %get-tuple-element.88), channel_id=1, source_target_pairs={{1,0},{2,1},{3,2},{4,3},{5,4},{6,5},{7,6},{9,8},{10,9},{11,10},{12... | collective-permute-start | bytes 3145736 | tf_op jit(solution)/shard_map/ppermute | solution.py:41
  583.4 186.1 %collective-permute-start.15 = (bf16[128,4096]{1,0:T(8,128)(2,1)}, bf16[128,4096]{1,0:T(8,128)(2,1)}, u32[]{:S(2)}, u32[]{:S(2)}) collective-permute-start(bf16[128,4096]{1,0:T(8,128)(2,1)} %get-tuple-element.89), channel_id=1, source_target_pairs={{3,0},{4,1},{5,2},{6,3},{7,4},{0,5},{1,6},{2,7},{11,8},{12,9},{13,... | collective-permute-start | bytes 3145736 | tf_op jit(solution)/shard_map/ppermute | solution.py:35
  583.5 187.7 %collective-permute-start.14 = (bf16[128,4096]{1,0:T(8,128)(2,1)}, bf16[128,4096]{1,0:T(8,128)(2,1)}, u32[]{:S(2)}, u32[]{:S(2)}) collective-permute-start(bf16[128,4096]{1,0:T(8,128)(2,1)} %get-tuple-element.90), channel_id=1, source_target_pairs={{5,0},{6,1},{7,2},{0,3},{1,4},{2,5},{3,6},{4,7},{13,8},{14,9},{15,... | collective-permute-start | bytes 3145736 | tf_op jit(solution)/shard_map/ppermute | solution.py:35
  586.1 182.4 %copy-start.1 = (bf16[2,128,2048]{1,2,0:T(8,128)(2,1)S(1)}, bf16[2,128,2048]{1,2,0:T(8,128)(2,1)}, u32[]{:S(2)}) copy-start(bf16[2,128,2048]{1,2,0:T(8,128)(2,1)} %copy-done) | copy-start | bytes 3145732
  586.1 182.4 %copy-start.7 = (bf16[2,16,128,128]{2,3,0,1:T(8,128)(2,1)S(1)}, bf16[2,16,128,128]{2,3,0,1:T(8,128)(2,1)}, u32[]{:S(2)}) copy-start(bf16[2,16,128,128]{2,3,0,1:T(8,128)(2,1)} %copy-done.6) | copy-start | bytes 3145732
  765.9 51.9 %collective-permute-start.13 = (bf16[128,4096]{1,0:T(8,128)(2,1)}, bf16[128,4096]{1,0:T(8,128)(2,1)}, u32[]{:S(2)}, u32[]{:S(2)}) collective-permute-start(bf16[128,4096]{1,0:T(8,128)(2,1)} %get-tuple-element.91), channel_id=1, source_target_pairs={{2,0},{3,1},{4,2},{5,3},{6,4},{7,5},{0,6},{1,7},{10,8},{11,9},{12,... | collective-permute-start | bytes 3145736 | tf_op jit(solution)/shard_map/ppermute | solution.py:35
  765.9 51.9 %collective-permute-start.12 = (bf16[128,4096]{1,0:T(8,128)(2,1)}, bf16[128,4096]{1,0:T(8,128)(2,1)}, u32[]{:S(2)}, u32[]{:S(2)}) collective-permute-start(bf16[128,4096]{1,0:T(8,128)(2,1)} %get-tuple-element.92), channel_id=1, source_target_pairs={{6,0},{7,1},{0,2},{1,3},{2,4},{3,5},{4,6},{5,7},{14,8},{15,9},{8,1... | collective-permute-start | bytes 3145736 | tf_op jit(solution)/shard_map/ppermute | solution.py:35
  769.4 66.5 %collective-permute-start.11 = (bf16[128,4096]{1,0:T(8,128)(2,1)}, bf16[128,4096]{1,0:T(8,128)(2,1)}, u32[]{:S(2)}, u32[]{:S(2)}) collective-permute-start(bf16[128,4096]{1,0:T(8,128)(2,1)} %get-tuple-element.93), channel_id=1, source_target_pairs={{1,0},{2,1},{3,2},{4,3},{5,4},{6,5},{7,6},{0,7},{9,8},{10,9},{11,1... | collective-permute-start | bytes 3145736 | tf_op jit(solution)/shard_map/ppermute | solution.py:35
  769.5 66.4 %collective-permute-start.10 = (bf16[128,4096]{1,0:T(8,128)(2,1)}, bf16[128,4096]{1,0:T(8,128)(2,1)}, u32[]{:S(2)}, u32[]{:S(2)}) collective-permute-start(bf16[128,4096]{1,0:T(8,128)(2,1)} %get-tuple-element.94), channel_id=1, source_target_pairs={{7,0},{0,1},{1,2},{2,3},{3,4},{4,5},{5,6},{6,7},{15,8},{8,9},{9,10... | collective-permute-start | bytes 3145736 | tf_op jit(solution)/shard_map/ppermute | solution.py:35
  771.2 74.1 %collective-permute-start.9 = (bf16[128,4096]{1,0:T(8,128)(2,1)}, bf16[128,4096]{1,0:T(8,128)(2,1)}, u32[]{:S(2)}, u32[]{:S(2)}) collective-permute-start(bf16[128,4096]{1,0:T(8,128)(2,1)} %get-tuple-element.95), channel_id=1, source_target_pairs={{0,1},{1,2},{2,3},{3,4},{4,5},{5,6},{6,7},{8,9},{9,10},{10,11},{11... | collective-permute-start | bytes 3145736 | tf_op jit(solution)/shard_map/ppermute | solution.py:41
  775.6 3.7 copy-start.15
Sparse Core Ops, SparseCore 0:
  28.6 206.7 all-reduce.10
  273.0 65.3 all-reduce.6
  389.8 62.3 all-gather.1
  564.2 200.4 all-reduce.8
  768.1 35.3 reduce-scatter.3
where the time goes:
time: 871 us; the launch traced here: 861 us
  blocking collectives  226 us (26%)
  starting transfers between devices  171 us (20%)
  local copies, waits for them, and re-layouts  155 us (18%)
  waiting for transfers between devices  122 us (14%)
  other arithmetic  101 us (12%)
  matrix products  71 us (8%)
  between operations  14.5 us (2%)
    psum x1, blocking collectives, on_device(): lax.psum((edge_query_part, pool_terms[per_device + 2:per_device + 4]), 's...  175 us
    ppermute x12, starting transfers between devices, from_behind(): return lax.ppermute(block, axis, route)  78.3 us
    ppermute x1, starting transfers between devices, extended(): lax.ppermute(lax.slice_in_dim(block, block.shape[dim] - width, None, axis...  76.7 us
    ppermute x12, waiting for transfers between devices, from_behind(): return lax.ppermute(block, axis, route)  65.7 us
    scatter-add x1, other arithmetic, on_device(): pool_terms = jnp.zeros((pool_count, BLOCK, 2 * width), jnp.float32).at[po...  41.9 us
    psum x1, blocking collectives, on_device(): lax.psum((jnp.sum(edge_exp, axis=3, keepdims=True), edge_part), 'seq')  26 us
    all_to_all x1, waiting for transfers between devices, on_device(): lax.all_to_all(split_up, 'seq', split_axis=2, concat_axis=0, tiled=True)  25.9 us
    pmax x1, blocking collectives, on_device(): edge_max = lax.pmax(jnp.max(edge_scores, axis=3, keepdims=True), 'seq')  25.4 us
  transfers between devices with their start and end apart: 22, of which 8 were waited for; matrix products, arithmetic and copies ran while one was open for 34% of the time, Pallas kernels for 0%

commit v1 on v0

v1 whole, which is shorter than its diff:
```python
import functools

import jax
import jax.numpy as jnp
from jax import lax
from jax.experimental import pallas as pl
from jax.experimental.pallas import tpu as pltpu
from jax.sharding import PartitionSpec as P

HD = 128
BLOCK = 128
MESH = pl.DeviceIdType.MESH
VMEM = pl.BlockSpec(memory_space=pltpu.VMEM)


def remote(src, dst, send_sem, recv_sem, **where):
    return pltpu.make_async_remote_copy(
        src_ref=src,
        dst_ref=dst,
        send_sem=send_sem,
        recv_sem=recv_sem,
        device_id=where,
        device_id_type=MESH,
    )


def greet(axes):
    barrier = pltpu.get_barrier_semaphore()
    count = 0
    for axis, size in axes:
        me = lax.axis_index(axis)
        for k in range(1, size):
            pl.semaphore_signal(
                barrier, inc=1, device_id={axis: lax.rem(me + k, size)}, device_id_type=MESH
            )
            count += 1
    pl.semaphore_wait(barrier, count)


def gather_kernel(
    n, proj_ref, up_ref, qkv_ref, u_ref, send, recv, r_send, r_recv, l_send, l_recv, p_send, p_recv,
    own_sem,
):
    me = lax.axis_index("seq")
    rows = proj_ref.shape[0]
    width = proj_ref.shape[1] // 3
    w = width // n
    chips = n // 2
    z = me // 2
    core = lax.rem(me, 2)
    partner = me + 1 - 2 * core

    def u_rows(index):
        return u_ref.at[pl.ds(pl.multiple_of(index * rows, rows), rows), :]

    def right(k, src):
        return remote(src, u_rows(me - 2 * k), r_send.at[k], r_recv.at[k], seq=me + 2)

    def left(k, src):
        return remote(src, u_rows(me + 2 * k), l_send.at[k], l_recv.at[k], seq=me - 2)

    def across(index, src):
        return remote(src, u_rows(index), p_send.at[index // 2], p_recv.at[index // 2], seq=partner)

    greet((("seq", n),))
    copies = []
    for k in range(1, n):
        p = lax.rem(me + k, n)
        for t in range(3):
            copy = remote(
                proj_ref.at[:, pl.ds(pl.multiple_of(t * width + p * w, w), w)],
                qkv_ref.at[t, pl.ds(pl.multiple_of(me * rows, rows), rows), :],
                send.at[t, k],
                recv.at[t, k],
                seq=p,
            )
            copy.start()
            copies.append(copy)

    @pl.when(z + 1 < chips)
    def _():
        right(0, up_ref).start()

    @pl.when(z >= 1)
    def _():
        left(0, up_ref).start()

    across(me, up_ref).start()
    owns = [
        pltpu.make_async_copy(
            proj_ref.at[:, pl.ds(pl.multiple_of(t * width + me * w, w), w)],
            qkv_ref.at[t, pl.ds(pl.multiple_of(me * rows, rows), rows), :],
            own_sem.at[t],
        )
        for t in range(3)
    ]
    owns.append(pltpu.make_async_copy(up_ref, u_rows(me), own_sem.at[3]))
    for copy in owns:
        copy.start()
    for k in range(1, chips):

        @pl.when(z - k >= 0)
        def _():
            right(k - 1, up_ref).wait_recv()
            block = me - 2 * k
            across(block, u_rows(block)).start()

            @pl.when(z + 1 < chips)
            def _():
                right(k, u_rows(block)).start()

        @pl.when(z + k < chips)
        def _():
            left(k - 1, up_ref).wait_recv()
            block = me + 2 * k
            across(block, u_rows(block)).start()

            @pl.when(z >= 1)
            def _():
                left(k, u_rows(block)).start()

    for copy in owns:
        copy.wait()
    for copy in copies:
        copy.wait()
    for i in range(chips):
        across(2 * i + core, up_ref).wait()
    for k in range(chips):

        @pl.when((z - k >= 0) & (z + 1 < chips))
        def _():
            right(k, up_ref).wait_send()

        @pl.when((z + k < chips) & (z >= 1))
        def _():
            left(k, up_ref).wait_send()


def gather(n, proj, up):
    rows, width3 = proj.shape
    w = width3 // 3 // n
    chips = n // 2
    dma = pltpu.SemaphoreType.DMA
    return pl.pallas_call(
        functools.partial(gather_kernel, n),
        out_shape=(
            jax.ShapeDtypeStruct((3, n * rows, w), proj.dtype),
            jax.ShapeDtypeStruct((n * rows, up.shape[1]), up.dtype),
        ),
        in_specs=[VMEM] * 2,
        out_specs=(VMEM, VMEM),
        scratch_shapes=[dma((3, n)), dma((3, n))] + [dma((chips,))] * 6 + [dma((4,))],
        compiler_params=pltpu.CompilerParams(collective_id=0, has_side_effects=True),
        name="gather",
    )(proj, up)


def attention_kernel(
    factor, q_ref, k_ref, v_ref, u_ref, w_ref, bias_ref, dq_ref, dk_ref, dv_ref, dw_ref,
    dk_acc, dv_acc, dw_acc,
):
    step = pl.program_id(1)
    scale = HD ** (-0.5)
    q, k, v = q_ref[0], k_ref[0], v_ref[0]
    length, tile = k.shape[0], q.shape[0]
    f32, bf16 = jnp.float32, jnp.bfloat16

    def dot(a, b, da, db):
        return lax.dot_general(a, b, (((da,), (db,)), ((), ())), preferred_element_type=f32)

    u = u_ref[pl.ds(pl.multiple_of(step * tile, tile), tile), :]
    grad_t = dot(w_ref[...], u, 1, 1).astype(bf16)
    grad_t32 = grad_t.astype(f32)
    grad = grad_t32.T.astype(bf16)
    blocks = bias_ref.shape[1]
    scores = dot(k, q, 1, 1) * scale
    scores = (scores.reshape(blocks, BLOCK, tile) + bias_ref[0][:, None, :]).reshape(length, tile)
    exponent = jnp.exp(scores - jnp.max(scores, axis=0, keepdims=True))
    inverse = 1.0 / jnp.sum(exponent, axis=0, keepdims=True)
    att = dot(v, exponent.astype(bf16), 0, 0) * inverse
    delta = jnp.sum(grad_t32 * att, axis=0, keepdims=True)
    probs = exponent * inverse
    score_grad = (probs * (dot(v, grad_t, 1, 0) - delta)).astype(bf16)
    dq_ref[...] = (dot(k, score_grad, 0, 0) * scale).T.astype(bf16)
    dk = dot(score_grad, q, 1, 0)
    dv = dot(probs.astype(bf16), grad, 1, 0)
    dw = dot(att.astype(bf16), u, 1, 0)

    @pl.when(step == 0)
    def _():
        dk_acc[...] = dk
        dv_acc[...] = dv
        dw_acc[...] = dw

    @pl.when(step > 0)
    def _():
        dk_acc[...] += dk
        dv_acc[...] += dv
        dw_acc[...] += dw

    @pl.when(step == pl.num_programs(1) - 1)
    def _():
        dk_ref[...] = (dk_acc[...] * scale).astype(bf16)
        dv_ref[...] = dv_acc[...].astype(bf16)
        dw_ref[...] = (dw_acc[...] * factor).astype(bf16)


def attention(factor, qkv, u_all, w_mine, bias):
    length, w = qkv.shape[1:]
    columns = u_all.shape[1]
    tile = min(2 * BLOCK, length)
    blocks = length // BLOCK
    bf16 = jnp.bfloat16
    bias_tiles = bias.reshape(blocks, length // tile, tile).transpose(1, 0, 2)
    return pl.pallas_call(
        functools.partial(attention_kernel, factor),
        grid=(w // HD, length // tile),
        out_shape=[jax.ShapeDtypeStruct((length, w), bf16)] * 3
        + [jax.ShapeDtypeStruct((w, columns), bf16)],
        in_specs=[
            pl.BlockSpec((1, tile, HD), lambda h, i: (0, i, h)),
            pl.BlockSpec((1, length, HD), lambda h, i: (1, 0, h)),
            pl.BlockSpec((1, length, HD), lambda h, i: (2, 0, h)),
            pl.BlockSpec((length, columns), lambda h, i: (0, 0)),
            pl.BlockSpec((HD, columns), lambda h, i: (h, 0)),
            pl.BlockSpec((1, blocks, tile), lambda h, i: (i, 0, 0)),
        ],
        out_specs=[
            pl.BlockSpec((tile, HD), lambda h, i: (i, h)),
            pl.BlockSpec((length, HD), lambda h, i: (0, h)),
            pl.BlockSpec((length, HD), lambda h, i: (0, h)),
            pl.BlockSpec((HD, columns), lambda h, i: (h, 0)),
        ],
        scratch_shapes=[
            pltpu.VMEM((length, HD), jnp.float32),
            pltpu.VMEM((length, HD), jnp.float32),
            pltpu.VMEM((HD, columns), jnp.float32),
        ],
        compiler_params=pltpu.CompilerParams(dimension_semantics=("arbitrary", "arbitrary")),
        name="attention",
    )(qkv, qkv, qkv, u_all, w_mine, bias_tiles)


def return_kernel(
    n, groups, dq_ref, dk_ref, dv_ref, dw_ref, grad_ref, out_ref, held, total, d_send, d_recv,
    send, recv, w_send, w_recv, own_sem,
):
    me, mine = lax.axis_index("seq"), lax.axis_index("dp")
    length, w = dq_ref.shape
    rows = length // n
    part = dw_ref.shape[1] // groups
    columns = part // n
    greet((("seq", n), ("dp", groups)))
    sums = []
    for k in range(1, groups):
        p = lax.rem(mine + k, groups)
        copy = remote(
            dw_ref.at[:, pl.ds(pl.multiple_of(p * part, part), part)],
            held.at[k - 1],
            d_send.at[k],
            d_recv.at[k],
            dp=p,
        )
        copy.start()
        sums.append(copy)
    copies = []
    place = [
        pl.ds(pl.multiple_of(t * n * w + me * w, w), w) for t in range(3)
    ]
    for k in range(1, n):
        p = lax.rem(me + k, n)
        for t, ref in enumerate((dq_ref, dk_ref, dv_ref)):
            copy = remote(
                ref.at[pl.ds(pl.multiple_of(p * rows, rows), rows), :],
                grad_ref.at[:, place[t]],
                send.at[t, k],
                recv.at[t, k],
                seq=p,
            )
            copy.start()
            copies.append(copy)
    owns = [
        pltpu.make_async_copy(
            ref.at[pl.ds(pl.multiple_of(me * rows, rows), rows), :],
            grad_ref.at[:, place[t]],
            own_sem.at[t],
        )
        for t, ref in enumerate((dq_ref, dk_ref, dv_ref))
    ]
    for copy in owns:
        copy.start()
    for copy in sums:
        copy.wait()
    summed = dw_ref[:, pl.ds(pl.multiple_of(mine * part, part), part)].astype(jnp.float32)
    for k in range(groups - 1):
        summed = summed + held[k].astype(jnp.float32)
    total[...] = summed.T.astype(total.dtype)

    def columns_of(p):
        return total.at[pl.ds(pl.multiple_of(p * columns, columns), columns), :]

    spot = out_ref.at[:, pl.ds(pl.multiple_of(me * w, w), w)]
    for k in range(1, n):
        p = lax.rem(me + k, n)
        copy = remote(columns_of(p), spot, w_send.at[k], w_recv.at[k], seq=p)
        copy.start()
        copies.append(copy)
    own = pltpu.make_async_copy(columns_of(me), spot, own_sem.at[3])
    own.start()
    for copy in owns + [own] + copies:
        copy.wait()


def give_back(n, groups, dq, dk, dv, dw):
    length, w = dq.shape
    part = dw.shape[1] // groups
    dma = pltpu.SemaphoreType.DMA
    return pl.pallas_call(
        functools.partial(return_kernel, n, groups),
        out_shape=(
            jax.ShapeDtypeStruct((length // n, 3 * n * w), dq.dtype),
            jax.ShapeDtypeStruct((part // n, n * w), dw.dtype),
        ),
        in_specs=[VMEM] * 4,
        out_specs=(VMEM, VMEM),
        scratch_shapes=[
            pltpu.VMEM((max(groups - 1, 1), w, part), dw.dtype),
            pltpu.VMEM((part, w), dw.dtype),
            dma((groups,)),
            dma((groups,)),
            dma((3, n)),
            dma((3, n)),
            dma((n,)),
            dma((n,)),
            dma((4,)),
        ],
        compiler_params=pltpu.CompilerParams(collective_id=1, has_side_effects=True),
        name="give_back",
    )(dq, dk, dv, dw)


def block_bias(partners, total):
    ids = jnp.arange(total, dtype=jnp.int32)
    chosen = jnp.any(partners[:, :, None] == ids[None, None, :], axis=1)
    near = jnp.abs(ids[:, None] - ids[None, :]) <= 1
    border = (ids == 0) | (ids == total - 1)
    linked = chosen | chosen.T | near | border[:, None] | border[None, :]
    return jnp.repeat(jnp.where(linked, 0.0, -1e30).astype(jnp.float32), BLOCK, axis=1)


def on_device(projected, upstream, w_out, partners):
    n, groups = lax.axis_size("seq"), lax.axis_size("dp")
    rows = projected.shape[1]
    w = w_out.shape[0] // n
    factor = (rows * n * groups) ** (-0.5)
    qkv, u_all = gather(n, projected[0], upstream[0])
    w_mine = lax.dynamic_slice_in_dim(w_out, lax.axis_index("seq") * w, w, 0)
    bias = block_bias(partners, rows * n // BLOCK)
    dq, dk, dv, dw = attention(factor, qkv, u_all, w_mine, bias)
    grad, dw_t = give_back(n, groups, dq, dk, dv, dw)
    return grad[None], dw_t.T.astype(jnp.float32)


def solution(mesh):
    return jax.shard_map(
        on_device,
        mesh=mesh,
        in_specs=(P("dp", "seq", None), P("dp", "seq", None), P(), P()),
        out_specs=(P("dp", "seq", None), P(None, ("dp", "seq"))),
        check_vma=False,
    )
```

time: 871 us -> 157 us (0.18)
  the two profiles are of different devices: /device:TPU:1 before, /device:TPU:29 now
where the time goes in v1:
time: 157 us; the launch traced here: 154 us
  Pallas kernels  145 us (92%)
  local copies, waits for them, and re-layouts  5.79 us (4%)
  other arithmetic  2.62 us (2%)
    pallas_call x1, Pallas kernels, gather(): pl.pallas_call(functools.partial(gather_kernel, n), out_shape=(jax.ShapeD...  79 us
    pallas_call x1, Pallas kernels, give_back(): pl.pallas_call(functools.partial(return_kernel, n, groups), out_shape=(ja...  46.3 us
    pallas_call x1, Pallas kernels, attention(): pl.pallas_call(functools.partial(attention_kernel, factor), grid=(w // HD...  20 us

profile of v1, /device:TPU:29, one launch (start us, length us, event | category | flops | bytes accessed | tf_op | source)
XLA Modules:
  0.0 154.4 jit_solution(3070832894933245192)
XLA Ops:
  0.6 0.8 fusion
  1.4 0.1 copy.11
  1.5 0.1 fusion.4
  1.6 0.1 broadcast_in_dim.22
  1.7 0.6 copy.14
  2.3 2.3 %constant_dynamic-slice_fusion.w_ref = bf16[256,2048]{1,0:T(8,128)(2,1)} fusion(bf16[2048,2048]{1,0:T(8,128)(2,1)} %param.6, s32[]{:T(128)S(6)} %select_n.7), kind=kLoop, calls=%fused_computation.11 | loop fusion | bytes 2097156 | tf_op jit(solution)/shard_map/dynamic_slice | solution.py:357
  4.6 79.0 %gather.1 = (bf16[3,1024,256]{2,1,0:T(8,128)(2,1)}, bf16[1024,2048]{1,0:T(8,128)(2,1)}) custom-call(bf16[128,6144]{1,0:T(8,128)(2,1)} %bitcast.13, bf16[128,2048]{1,0:T(8,128)(2,1)} %bitcast.14), custom_call_target="tpu_custom_call" | custom-call | tf_op jit(solution)/shard_map/gather/pallas_call | solution.py:144
  83.6 20.0 %attention.1 = (bf16[1024,256]{1,0:T(8,128)(2,1)}, bf16[1024,256]{1,0:T(8,128)(2,1)}, bf16[1024,256]{1,0:T(8,128)(2,1)}, bf16[256,2048]{1,0:T(8,128)(2,1)}) custom-call(bf16[3,1024,256]{2,1,0:T(8,128)(2,1)} %get-tuple-element.10.q_ref.k_ref.v_ref, bf16[3,1024,256]{2,1,0:T(8,128)(2,1)} %get-tuple-element.10.q_ref.k_ref.v_ref, ...), custom_call_target="tpu_custom_call" | custom-call | tf_op jit(solution)/shard_map/attention/pallas_call | solution.py:215
  103.6 46.3 %give_back.1 = (bf16[128,6144]{1,0:T(8,128)(2,1)}, bf16[64,2048]{1,0:T(8,128)(2,1)}) custom-call(bf16[1024,256]{1,0:T(8,128)(2,1)} %get-tuple-element.12.dq_ref, bf16[1024,256]{1,0:T(8,128)(2,1)} %get-tuple-element.13.dk_ref, bf16[1024,256]{1,0:T(8,128)(2,1)} %get-tuple-element.14.dv_ref, bf16[256,2048]{1,0:T(8,128)(2,1)} %get-tuple-element.15.dw_ref), custom_call_target="tpu_custom_call" | custom-call | tf_op jit(solution)/shard_map/give_back/pallas_call | solution.py:318
  149.9 1.8 %convert_bitcast_fusion = f32[2048,64]{0,1:T(8,128)} fusion(bf16[64,2048]{1,0:T(8,128)(2,1)} %get-tuple-element.17), kind=kLoop, calls=%fused_computation | loop fusion | flops 131072 | bytes 786432 | tf_op jit(solution)/shard_map/convert_element_type | solution.py:361
  151.7 2.7 %copy.16 = bf16[1,128,6144]{2,1,0:T(8,128)(2,1)} copy(bf16[1,128,6144]{2,1,0:T(8,128)(2,1)} %bitcast.12) | data formatting | bytes 3145728
  (2 shorter events, 0.0 us)

commit v2 on v1

v2 whole, which is shorter than its diff:
```python
import functools

import jax
import jax.numpy as jnp
from jax import lax
from jax.experimental import pallas as pl
from jax.experimental.pallas import tpu as pltpu
from jax.sharding import PartitionSpec as P

HD = 128
BLOCK = 128
MESH = pl.DeviceIdType.MESH
VMEM = pl.BlockSpec(memory_space=pltpu.VMEM)


def remote(src, dst, send_sem, recv_sem, **where):
    return pltpu.make_async_remote_copy(
        src_ref=src,
        dst_ref=dst,
        send_sem=send_sem,
        recv_sem=recv_sem,
        device_id=where,
        device_id_type=MESH,
    )


def greet(axes):
    barrier = pltpu.get_barrier_semaphore()
    count = 0
    for axis, size in axes:
        me = lax.axis_index(axis)
        for k in range(1, size):
            pl.semaphore_signal(
                barrier, inc=1, device_id={axis: lax.rem(me + k, size)}, device_id_type=MESH
            )
            count += 1
    pl.semaphore_wait(barrier, count)


def layer_kernel(
    n, groups, factor, proj_ref, up_ref, bias_ref, w_ref, grad_ref, out_ref, qkv, u_all, w_mine,
    og, kt, vt, dk_acc, dv_acc, dw_acc, grads, terms, held, total, q_send, q_recv, r_send, r_recv,
    l_send, l_recv, p_send, p_recv, g_send, g_recv, d_send, d_recv, w_send, w_recv, own_sem,
    own_q, own_g, own_w,
):
    me, mine = lax.axis_index("seq"), lax.axis_index("dp")
    rows = proj_ref.shape[0]
    width = proj_ref.shape[1] // 3
    length = n * rows
    heads = width // HD // n
    part = up_ref.shape[1] // groups
    columns = part // n
    chips = n // 2
    z = me // 2
    core = lax.rem(me, 2)
    partner = me + 1 - 2 * core
    scale = HD ** (-0.5)
    f32, bf16 = jnp.float32, jnp.bfloat16
    tile = min(2 * BLOCK, length)

    def dot(a, b, da, db):
        return lax.dot_general(a, b, (((da,), (db,)), ((), ())), preferred_element_type=f32)

    def span(index, size):
        return pl.ds(pl.multiple_of(index * size, size), size)

    def u_rows(index):
        return u_all.at[span(index, rows), :]

    def right(k, src):
        return remote(src, u_rows(me - 2 * k), r_send.at[k], r_recv.at[k], seq=me + 2)

    def left(k, src):
        return remote(src, u_rows(me + 2 * k), l_send.at[k], l_recv.at[k], seq=me - 2)

    def across(index, src):
        return remote(src, u_rows(index), p_send.at[index // 2], p_recv.at[index // 2], seq=partner)

    def head_columns(t, device, h):
        return span(t * n * heads + device * heads + h, HD)

    def send_head(h):
        started = []
        for k in range(1, n):
            p = lax.rem(me + k, n)
            for t in range(3):
                copy = remote(
                    proj_ref.at[:, head_columns(t, p, h)],
                    qkv.at[h, t, span(me, rows), :],
                    q_send.at[h, t, k],
                    q_recv.at[h, t, k],
                    seq=p,
                )
                copy.start()
                started.append(copy)
        for t in range(3):
            copy = pltpu.make_async_copy(
                proj_ref.at[:, head_columns(t, me, h)],
                qkv.at[h, t, span(me, rows), :],
                own_q.at[h, t],
            )
            copy.start()
            started.append(copy)
        return started

    load_w = pltpu.make_async_copy(w_ref.at[span(me, heads * HD), :], w_mine, own_sem.at[0])
    load_w.start()
    greet((("seq", n), ("dp", groups)))

    @pl.when(z + 1 < chips)
    def _():
        right(0, up_ref).start()

    @pl.when(z >= 1)
    def _():
        left(0, up_ref).start()

    across(me, up_ref).start()
    own_u = pltpu.make_async_copy(up_ref, u_rows(me), own_sem.at[1])
    own_u.start()
    arriving = []
    for k in range(1, chips):

        @pl.when(z - k >= 0)
        def _():
            right(k - 1, up_ref).wait_recv()
            block = me - 2 * k

            @pl.when(z + 1 < chips)
            def _():
                right(k, u_rows(block)).start()

            across(block, u_rows(block)).start()

        @pl.when(z + k < chips)
        def _():
            left(k - 1, up_ref).wait_recv()
            block = me + 2 * k

            @pl.when(z >= 1)
            def _():
                left(k, u_rows(block)).start()

            across(block, u_rows(block)).start()

        if len(arriving) < heads:
            arriving.append(send_head(len(arriving)))
    while len(arriving) < heads:
        arriving.append(send_head(len(arriving)))
    load_w.wait()
    own_u.wait()
    for i in range(chips):
        across(2 * i + core, up_ref).wait_recv()

    def out_grad_step(i, carry):
        u = u_all[span(i, tile), :]
        og[:, span(i, tile)] = dot(w_mine[...], u, 1, 1).astype(bf16)
        return carry

    lax.fori_loop(0, length // tile, out_grad_step, 0)
    leaving = []
    sums = []
    for h in range(heads):
        for copy in arriving[h]:
            copy.wait()
        kt[...] = qkv[h, 1].astype(f32).T.astype(bf16)
        vt[...] = qkv[h, 2].astype(f32).T.astype(bf16)
        dk_acc[...] = jnp.zeros_like(dk_acc)
        dv_acc[...] = jnp.zeros_like(dv_acc)
        dw_acc[...] = jnp.zeros_like(dw_acc)

        def tile_step(i, carry):
            at = span(i, tile)
            q, k, v = qkv[h, 0, at, :], qkv[h, 1], qkv[h, 2]
            grad_t = og[h * HD : (h + 1) * HD, at]
            grad_t32 = grad_t.astype(f32)
            scores = dot(k, q, 1, 1) * scale
            scores = scores.reshape(length // BLOCK, BLOCK, tile) + bias_ref[:, at][:, None, :]
            scores = scores.reshape(length, tile)
            exponent = jnp.exp(scores - jnp.max(scores, axis=0, keepdims=True))
            inverse = 1.0 / jnp.sum(exponent, axis=0, keepdims=True)
            att = dot(vt[...], exponent.astype(bf16), 1, 0) * inverse
            delta = jnp.sum(grad_t32 * att, axis=0, keepdims=True)
            probs = exponent * inverse
            score_grad = (probs * (dot(v, grad_t, 1, 0) - delta)).astype(bf16)
            grads[h, 0, at, :] = (dot(kt[...], score_grad, 1, 0) * scale).T.astype(bf16)
            dk_acc[...] += dot(score_grad, q, 1, 0)
            dv_acc[...] += dot(probs.astype(bf16), grad_t32.T.astype(bf16), 1, 0)
            dw_acc[...] += dot(att.astype(bf16), u_all[at, :], 1, 0)
            return carry

        lax.fori_loop(0, length // tile, tile_step, 0)
        terms[h] = (dw_acc[...] * factor).astype(bf16)
        for k in range(1, groups):
            p = lax.rem(mine + k, groups)
            copy = remote(
                terms.at[h, :, span(p, part)],
                held.at[h, k - 1],
                d_send.at[h, k],
                d_recv.at[h, k],
                dp=p,
            )
            copy.start()
            sums.append(copy)
        grads[h, 1] = (dk_acc[...] * scale).astype(bf16)
        grads[h, 2] = dv_acc[...].astype(bf16)
        for k in range(1, n):
            p = lax.rem(me + k, n)
            for t in range(3):
                copy = remote(
                    grads.at[h, t, span(p, rows), :],
                    grad_ref.at[:, head_columns(t, me, h)],
                    g_send.at[h, t, k],
                    g_recv.at[h, t, k],
                    seq=p,
                )
                copy.start()
                leaving.append(copy)
        for t in range(3):
            copy = pltpu.make_async_copy(
                grads.at[h, t, span(me, rows), :],
                grad_ref.at[:, head_columns(t, me, h)],
                own_g.at[h, t],
            )
            copy.start()
            leaving.append(copy)
    for copy in sums:
        copy.wait()
    for h in range(heads):
        summed = terms[h, :, span(mine, part)].astype(f32)
        for k in range(groups - 1):
            summed = summed + held[h, k].astype(f32)
        total[h] = summed.T.astype(bf16)
        spot = out_ref.at[:, span(me * heads + h, HD)]
        for k in range(1, n):
            p = lax.rem(me + k, n)
            copy = remote(
                total.at[h, span(p, columns), :], spot, w_send.at[h, k], w_recv.at[h, k], seq=p
            )
            copy.start()
            leaving.append(copy)
        copy = pltpu.make_async_copy(total.at[h, span(me, columns), :], spot, own_w.at[h])
        copy.start()
        leaving.append(copy)
    for copy in leaving:
        copy.wait()
    for i in range(chips):
        across(2 * i + core, up_ref).wait_send()
    for k in range(chips):

        @pl.when((z - k >= 0) & (z + 1 < chips))
        def _():
            right(k, up_ref).wait_send()

        @pl.when((z + k < chips) & (z >= 1))
        def _():
            left(k, up_ref).wait_send()


def layer(n, groups, factor, proj, up, bias, w_out):
    rows, width3 = proj.shape
    width = width3 // 3
    heads = width // HD // n
    length, depth = n * rows, up.shape[1]
    part = depth // groups
    chips = n // 2
    f32, bf16 = jnp.float32, jnp.bfloat16
    dma = pltpu.SemaphoreType.DMA
    return pl.pallas_call(
        functools.partial(layer_kernel, n, groups, factor),
        out_shape=(
            jax.ShapeDtypeStruct((rows, width3), bf16),
            jax.ShapeDtypeStruct((part // n, width), bf16),
        ),
        in_specs=[VMEM] * 3 + [pl.BlockSpec(memory_space=pl.ANY)],
        out_specs=(VMEM, VMEM),
        scratch_shapes=[
            pltpu.VMEM((heads, 3, length, HD), bf16),
            pltpu.VMEM((length, depth), bf16),
            pltpu.VMEM((heads * HD, depth), bf16),
            pltpu.VMEM((heads * HD, length), bf16),
            pltpu.VMEM((HD, length), bf16),
            pltpu.VMEM((HD, length), bf16),
            pltpu.VMEM((length, HD), f32),
            pltpu.VMEM((length, HD), f32),
            pltpu.VMEM((HD, depth), f32),
            pltpu.VMEM((heads, 3, length, HD), bf16),
            pltpu.VMEM((heads, HD, depth), bf16),
            pltpu.VMEM((heads, max(groups - 1, 1), HD, part), bf16),
            pltpu.VMEM((heads, part, HD), bf16),
            dma((heads, 3, n)),
            dma((heads, 3, n)),
        ]
        + [dma((chips,))] * 6
        + [
            dma((heads, 3, n)),
            dma((heads, 3, n)),
            dma((heads, groups)),
            dma((heads, groups)),
            dma((heads, n)),
            dma((heads, n)),
            dma((2,)),
            dma((heads, 3)),
            dma((heads, 3)),
            dma((heads,)),
        ],
        compiler_params=pltpu.CompilerParams(
            collective_id=0, has_side_effects=True, vmem_limit_bytes=60 * 2**20
        ),
        name="layer",
    )(proj, up, bias, w_out)


def block_bias(partners, total):
    ids = jnp.arange(total, dtype=jnp.int32)
    chosen = jnp.any(partners[:, :, None] == ids[None, None, :], axis=1)
    near = jnp.abs(ids[:, None] - ids[None, :]) <= 1
    border = (ids == 0) | (ids == total - 1)
    linked = chosen | chosen.T | near | border[:, None] | border[None, :]
    return jnp.repeat(jnp.where(linked, 0.0, -1e30).astype(jnp.float32), BLOCK, axis=1)


def on_device(projected, upstream, w_out, partners):
    n, groups = lax.axis_size("seq"), lax.axis_size("dp")
    rows = projected.shape[1]
    factor = (rows * n * groups) ** (-0.5)
    bias = block_bias(partners, rows * n // BLOCK)
    grad, dw_t = layer(n, groups, factor, projected[0], upstream[0], bias, w_out)
    return grad[None], dw_t.T.astype(jnp.float32)


def solution(mesh):
    return jax.shard_map(
        on_device,
        mesh=mesh,
        in_specs=(P("dp", "seq", None), P("dp", "seq", None), P(), P()),
        out_specs=(P("dp", "seq", None), P(None, ("dp", "seq"))),
        check_vma=False,
    )
```

time: 157 us -> 126 us (0.80); the launches traced: 154 us -> 126 us
  Pallas kernels: 145 us -> 119 us
  local copies, waits for them, and re-layouts: 5.79 us -> 3.54 us
    pallas_call x3 -> x1, Pallas kernels: 145 us -> 119 us  [layer(): pl.pallas_call(functools.partial(layer_kernel, n, groups, factor), out_sh...]
    dynamic_slice x1 -> x0, local copies, waits for them, and re-layouts: 2.3 us -> none  [on_device(): w_mine = lax.dynamic_slice_in_dim(w_out, lax.axis_index('seq') * w, w, 0)]
where the time goes in v2:
time: 126 us
  Pallas kernels  119 us (94%)
  local copies, waits for them, and re-layouts  3.54 us (3%)
  other arithmetic  2.62 us (2%)
    pallas_call x1, Pallas kernels, layer(): pl.pallas_call(functools.partial(layer_kernel, n, groups, factor), out_sh...  119 us
    unnamed x1, local copies, waits for them, and re-layouts  2.69 us

profile of v2, /device:TPU:29, one launch (start us, length us, event | category | flops | bytes accessed | tf_op | source)
XLA Modules:
  0.0 126.1 jit_solution(15738742160862975643)
XLA Ops:
  0.6 0.8 fusion
  1.4 0.1 copy.8
  1.5 0.1 fusion.4
  1.6 0.1 copy.9
  1.6 0.7 broadcast_bitcast_fusion.bias_ref
  2.3 119.3 %layer.1 = (bf16[128,6144]{1,0:T(8,128)(2,1)}, bf16[64,2048]{1,0:T(8,128)(2,1)}) custom-call(bf16[128,6144]{1,0:T(8,128)(2,1)} %bitcast.11, bf16[128,2048]{1,0:T(8,128)(2,1)} %bitcast.13, f32[8,1024]{1,0:T(8,128)} %broadcast_bitcast_fusion.bias_ref, bf16[2048,2048]{1,0:T(8,128)(2,1)} %w_ref.1), custom_call_target="tpu_custom_call" | custom-call | tf_op jit(solution)/shard_map/layer/pallas_call | solution.py:269
  121.6 1.8 %convert_bitcast_fusion = f32[2048,64]{0,1:T(8,128)} fusion(bf16[64,2048]{1,0:T(8,128)(2,1)} %get-tuple-element.5), kind=kLoop, calls=%fused_computation | loop fusion | flops 131072 | bytes 786432 | tf_op jit(solution)/shard_map/convert_element_type | solution.py:329
  123.4 2.7 %copy.11 = bf16[1,128,6144]{2,1,0:T(8,128)(2,1)} copy(bf16[1,128,6144]{2,1,0:T(8,128)(2,1)} %bitcast.12) | data formatting | bytes 3145728
  (1 shorter events, 0.0 us)

commit v3 on v2

--- a/solution.py
+++ b/solution.py
@@ -9,6 +9,7 @@
 
 HD = 128
 BLOCK = 128
+PIECES = 4
 MESH = pl.DeviceIdType.MESH
 VMEM = pl.BlockSpec(memory_space=pltpu.VMEM)
 
@@ -64,17 +65,23 @@
     def span(index, size):
         return pl.ds(pl.multiple_of(index * size, size), size)
 
-    def u_rows(index):
-        return u_all.at[span(index, rows), :]
-
-    def right(k, src):
-        return remote(src, u_rows(me - 2 * k), r_send.at[k], r_recv.at[k], seq=me + 2)
-
-    def left(k, src):
-        return remote(src, u_rows(me + 2 * k), l_send.at[k], l_recv.at[k], seq=me - 2)
-
-    def across(index, src):
-        return remote(src, u_rows(index), p_send.at[index // 2], p_recv.at[index // 2], seq=partner)
+    size = rows // PIECES
+
+    def u_rows(index, j):
+        return u_all.at[pl.ds(pl.multiple_of(index * rows + j * size, size), size), :]
+
+    def mine_rows(j):
+        return up_ref.at[j * size : (j + 1) * size, :]
+
+    def right(k, j, src):
+        return remote(src, u_rows(me - 2 * k, j), r_send.at[k, j], r_recv.at[k, j], seq=me + 2)
+
+    def left(k, j, src):
+        return remote(src, u_rows(me + 2 * k, j), l_send.at[k, j], l_recv.at[k, j], seq=me - 2)
+
+    def across(index, j, src):
+        spot = index // 2
+        return remote(src, u_rows(index, j), p_send.at[spot, j], p_recv.at[spot, j], seq=partner)
 
     def head_columns(t, device, h):
         return span(t * n * heads + device * heads + h, HD)
@@ -107,50 +114,55 @@
     load_w.start()
     greet((("seq", n), ("dp", groups)))
 
-    @pl.when(z + 1 < chips)
-    def _():
-        right(0, up_ref).start()
-
-    @pl.when(z >= 1)
-    def _():
-        left(0, up_ref).start()
-
-    across(me, up_ref).start()
-    own_u = pltpu.make_async_copy(up_ref, u_rows(me), own_sem.at[1])
+    for j in range(PIECES):
+
+        @pl.when(z + 1 < chips)
+        def _():
+            right(0, j, mine_rows(j)).start()
+
+        @pl.when(z >= 1)
+        def _():
+            left(0, j, mine_rows(j)).start()
+
+    for j in range(PIECES):
+        across(me, j, mine_rows(j)).start()
+    own_u = pltpu.make_async_copy(up_ref, u_all.at[span(me, rows), :], own_sem.at[1])
     own_u.start()
     arriving = []
     for k in range(1, chips):
-
-        @pl.when(z - k >= 0)
-        def _():
-            right(k - 1, up_ref).wait_recv()
-            block = me - 2 * k
-
-            @pl.when(z + 1 < chips)
+        while len(arriving) < min(heads, k - 1):
+            arriving.append(send_head(len(arriving)))
+        for j in range(PIECES):
+
+            @pl.when(z - k >= 0)
             def _():
-                right(k, u_rows(block)).start()
-
-            across(block, u_rows(block)).start()
-
-        @pl.when(z + k < chips)
-        def _():
-            left(k - 1, up_ref).wait_recv()
-            block = me + 2 * k
-
-            @pl.when(z >= 1)
+                right(k - 1, j, mine_rows(j)).wait_recv()
+                block = me - 2 * k
+
+                @pl.when(z + 1 < chips)
+                def _():
+                    right(k, j, u_rows(block, j)).start()
+
+                across(block, j, u_rows(block, j)).start()
+
+            @pl.when(z + k < chips)
             def _():
-                left(k, u_rows(block)).start()
-
-            across(block, u_rows(block)).start()
-
-        if len(arriving) < heads:
-            arriving.append(send_head(len(arriving)))
+                left(k - 1, j, mine_rows(j)).wait_recv()
+                block = me + 2 * k
+
+                @pl.when(z >= 1)
+                def _():
+                    left(k, j, u_rows(block, j)).start()
+
+                across(block, j, u_rows(block, j)).start()
+
     while len(arriving) < heads:
         arriving.append(send_head(len(arriving)))
     load_w.wait()
     own_u.wait()
     for i in range(chips):
-        across(2 * i + core, up_ref).wait_recv()
+        for j in range(PIECES):
+            across(2 * i + core, j, mine_rows(j)).wait_recv()
 
     def out_grad_step(i, carry):
         u = u_all[span(i, tile), :]
@@ -244,17 +256,18 @@
         leaving.append(copy)
     for copy in leaving:
         copy.wait()
-    for i in range(chips):
-        across(2 * i + core, up_ref).wait_send()
-    for k in range(chips):
-
-        @pl.when((z - k >= 0) & (z + 1 < chips))
-        def _():
-            right(k, up_ref).wait_send()
-
-        @pl.when((z + k < chips) & (z >= 1))
-        def _():
-            left(k, up_ref).wait_send()
+    for j in range(PIECES):
+        for i in range(chips):
+            across(2 * i + core, j, mine_rows(j)).wait_send()
+        for k in range(chips):
+
+            @pl.when((z - k >= 0) & (z + 1 < chips))
+            def _():
+                right(k, j, mine_rows(j)).wait_send()
+
+            @pl.when((z + k < chips) & (z >= 1))
+            def _():
+                left(k, j, mine_rows(j)).wait_send()
 
 
 def layer(n, groups, factor, proj, up, bias, w_out):
@@ -291,7 +304,7 @@
             dma((heads, 3, n)),
             dma((heads, 3, n)),
         ]
-        + [dma((chips,))] * 6
+        + [dma((chips, PIECES))] * 6
         + [
             dma((heads, 3, n)),
             dma((heads, 3, n)),

time: 126 us -> 118 us (0.937)
  Pallas kernels: 119 us -> 111 us
    pallas_call x1, Pallas kernels: 119 us -> 111 us  [layer(): pl.pallas_call(functools.partial(layer_kernel, n, groups, factor), out_sh...]
where the time goes in v3:
time: 118 us
  Pallas kernels  111 us (94%)
  local copies, waits for them, and re-layouts  3.54 us (3%)
  other arithmetic  2.62 us (2%)
    pallas_call x1, Pallas kernels, layer(): pl.pallas_call(functools.partial(layer_kernel, n, groups, factor), out_sh...  111 us
    unnamed x1, local copies, waits for them, and re-layouts  2.69 us

profile of v3, /device:TPU:29, one launch (start us, length us, event | category | flops | bytes accessed | tf_op | source)
XLA Modules:
  0.0 117.9 jit_solution(9382137241115102252)
XLA Ops:
  0.6 0.8 fusion
  1.4 0.1 copy.8
  1.5 0.1 fusion.4
  1.6 0.1 copy.9
  1.6 0.7 broadcast_bitcast_fusion.bias_ref
  2.3 111.1 %layer.1 = (bf16[128,6144]{1,0:T(8,128)(2,1)}, bf16[64,2048]{1,0:T(8,128)(2,1)}) custom-call(bf16[128,6144]{1,0:T(8,128)(2,1)} %bitcast.11, bf16[128,2048]{1,0:T(8,128)(2,1)} %bitcast.13, f32[8,1024]{1,0:T(8,128)} %broadcast_bitcast_fusion.bias_ref, bf16[2048,2048]{1,0:T(8,128)(2,1)} %w_ref.1), custom_call_target="tpu_custom_call" | custom-call | tf_op jit(solution)/shard_map/layer/pallas_call | solution.py:282
  113.4 1.8 %convert_bitcast_fusion = f32[2048,64]{0,1:T(8,128)} fusion(bf16[64,2048]{1,0:T(8,128)(2,1)} %get-tuple-element.5), kind=kLoop, calls=%fused_computation | loop fusion | flops 131072 | bytes 786432 | tf_op jit(solution)/shard_map/convert_element_type | solution.py:342
  115.2 2.7 %copy.11 = bf16[1,128,6144]{2,1,0:T(8,128)(2,1)} copy(bf16[1,128,6144]{2,1,0:T(8,128)(2,1)} %bitcast.12) | data formatting | bytes 3145728
  (1 shorter events, 0.0 us)

commit v4 on v3

--- a/solution.py
+++ b/solution.py
@@ -172,6 +172,26 @@
     lax.fori_loop(0, length // tile, out_grad_step, 0)
     leaving = []
     sums = []
+
+    def finish(h):
+        for copy in sums[h]:
+            copy.wait()
+        summed = terms[h, :, span(mine, part)].astype(f32)
+        for k in range(groups - 1):
+            summed = summed + held[h, k].astype(f32)
+        total[h] = summed.T.astype(bf16)
+        spot = out_ref.at[:, span(me * heads + h, HD)]
+        for k in range(1, n):
+            p = lax.rem(me + k, n)
+            copy = remote(
+                total.at[h, span(p, columns), :], spot, w_send.at[h, k], w_recv.at[h, k], seq=p
+            )
+            copy.start()
+            leaving.append(copy)
+        copy = pltpu.make_async_copy(total.at[h, span(me, columns), :], spot, own_w.at[h])
+        copy.start()
+        leaving.append(copy)
+
     for h in range(heads):
         for copy in arriving[h]:
             copy.wait()
@@ -202,6 +222,7 @@
             return carry
 
         lax.fori_loop(0, length // tile, tile_step, 0)
+        sums.append([])
         terms[h] = (dw_acc[...] * factor).astype(bf16)
         for k in range(1, groups):
             p = lax.rem(mine + k, groups)
@@ -213,7 +234,9 @@
                 dp=p,
             )
             copy.start()
-            sums.append(copy)
+            sums[h].append(copy)
+        if h > 0:
+            finish(h - 1)
         grads[h, 1] = (dk_acc[...] * scale).astype(bf16)
         grads[h, 2] = dv_acc[...].astype(bf16)
         for k in range(1, n):
@@ -236,24 +259,7 @@
             )
             copy.start()
             leaving.append(copy)
-    for copy in sums:
-        copy.wait()
-    for h in range(heads):
-        summed = terms[h, :, span(mine, part)].astype(f32)
-        for k in range(groups - 1):
-            summed = summed + held[h, k].astype(f32)
-        total[h] = summed.T.astype(bf16)
-        spot = out_ref.at[:, span(me * heads + h, HD)]
-        for k in range(1, n):
-            p = lax.rem(me + k, n)
-            copy = remote(
-                total.at[h, span(p, columns), :], spot, w_send.at[h, k], w_recv.at[h, k], seq=p
-            )
-            copy.start()
-            leaving.append(copy)
-        copy = pltpu.make_async_copy(total.at[h, span(me, columns), :], spot, own_w.at[h])
-        copy.start()
-        leaving.append(copy)
+    finish(heads - 1)
     for copy in leaving:
         copy.wait()
     for j in range(PIECES):

time: 118 us -> 118 us (level)
  no operation moved by 1% of the time
where the time goes in v4:
time: 118 us
  Pallas kernels  111 us (94%)
  local copies, waits for them, and re-layouts  3.54 us (3%)
  other arithmetic  2.62 us (2%)
    pallas_call x1, Pallas kernels, layer(): pl.pallas_call(functools.partial(layer_kernel, n, groups, factor), out_sh...  111 us
    unnamed x1, local copies, waits for them, and re-layouts  2.69 us

profile of v4, /device:TPU:29, one launch (start us, length us, event | category | flops | bytes accessed | tf_op | source)
XLA Modules:
  0.0 118.0 jit_solution(9664654774012371548)
XLA Ops:
  0.6 0.8 fusion
  1.4 0.1 copy.8
  1.5 0.1 fusion.4
  1.6 0.1 copy.9
  1.6 0.7 broadcast_bitcast_fusion.bias_ref
  2.3 111.2 %layer.1 = (bf16[128,6144]{1,0:T(8,128)(2,1)}, bf16[64,2048]{1,0:T(8,128)(2,1)}) custom-call(bf16[128,6144]{1,0:T(8,128)(2,1)} %bitcast.11, bf16[128,2048]{1,0:T(8,128)(2,1)} %bitcast.13, f32[8,1024]{1,0:T(8,128)} %broadcast_bitcast_fusion.bias_ref, bf16[2048,2048]{1,0:T(8,128)(2,1)} %w_ref.1), custom_call_target="tpu_custom_call" | custom-call | tf_op jit(solution)/shard_map/layer/pallas_call | solution.py:288
  113.5 1.8 %convert_bitcast_fusion = f32[2048,64]{0,1:T(8,128)} fusion(bf16[64,2048]{1,0:T(8,128)(2,1)} %get-tuple-element.5), kind=kLoop, calls=%fused_computation | loop fusion | flops 131072 | bytes 786432 | tf_op jit(solution)/shard_map/convert_element_type | solution.py:348
  115.3 2.7 %copy.11 = bf16[1,128,6144]{2,1,0:T(8,128)(2,1)} copy(bf16[1,128,6144]{2,1,0:T(8,128)(2,1)} %bitcast.12) | data formatting | bytes 3145728
  (1 shorter events, 0.0 us)
